TPU v7x, 256 devices: a whole 4x4x8 slice. The times are simulated.
256 devices in a mesh: grp: 8 (over z_hi, core), mem: 32 (over y, x, z_lo).
Axes of the slice: x: 4, y: 4, z: 8 (z_hi: 4, z_lo: 2; z = z_hi * 2 + z_lo), core: 2. Of those that a mesh axis runs over, the one named last changes fastest.
Arguments:
- spectra: bfloat16 [3072, 64, 384], P(('grp', 'mem')), may hold values from -45 to 45
Outputs:
- correlations: bfloat16 [7, 8, 384, 32, 12, 128], P(None, 'grp', None, 'mem')
All inputs are finite; a program needn't handle non-finite values.
Results may differ from a plain program's by a relative error of at most 0.0067.
Values may be sent and summed in bfloat16 or wider, within the bound.
No kernel may reach another device: no remote copies, remote signals or barrier semaphores. Data moves between devices by JAX's collectives and lax.ppermute only.
A program may use at most 128 MiB of HBM per device.

v0:
```python
import math
import jax
import jax.numpy as jnp
from jax import lax
from jax.sharding import PartitionSpec as P


def whiten(spectra):
    values = spectra.astype(jnp.float32)
    windows = values.shape[-1] // 2
    power_sum = values[..., :windows] ** 2 + values[..., windows:] ** 2
    amplitude = jnp.sqrt(jnp.mean(power_sum, axis=1, keepdims=True) + 1e-06)
    divisor = jnp.concatenate([amplitude, amplitude], -1)
    return (values / divisor).astype(jnp.bfloat16)


def lag_table(bin_count, lag_count):
    freq_index = jnp.arange(bin_count, dtype=jnp.int32)
    lag_index = jnp.arange(lag_count, dtype=jnp.int32)
    product = freq_index[:, None] * lag_index[None, :] % lag_count
    phase = product.astype(jnp.float32) * (2.0 * math.pi / lag_count)
    weight = 1.0 / math.sqrt(bin_count)
    return (jnp.stack([jnp.cos(phase), -jnp.sin(phase)]) * weight).astype(jnp.bfloat16)


def round_partners(group_count):
    last_label = group_count - 1
    round_label = jnp.arange(last_label, dtype=jnp.int32)[:, None]
    label_index = jnp.arange(group_count, dtype=jnp.int32)[None, :]
    opposite = jnp.mod(2 * round_label - label_index, last_label)
    inner = jnp.where(opposite == label_index, last_label, opposite)
    return jnp.where(label_index == last_label, round_label, inner)


def with_rotation(partner_blocks, windows, axis_at):
    rotated = jnp.concatenate([-partner_blocks[..., windows:], partner_blocks[..., :windows]], -1)
    return jnp.stack([partner_blocks, rotated], axis_at)


def shards(spectra):
    white = whiten(spectra)
    block_rows, bin_count, width_total = white.shape
    windows = width_total // 2
    norm_scale = 1.0 / math.sqrt(windows)
    lag_count = 2 * bin_count
    table = lag_table(bin_count, lag_count)
    pairing = round_partners(lax.axis_size("grp"))
    group_index = lax.axis_index("grp")
    partners = jnp.take(pairing, group_index, axis=1)
    collected = lax.all_gather(white, "grp", axis=0, tiled=True)
    collected = collected.reshape(-1, block_rows, bin_count, width_total)
    partner_blocks = jnp.take(collected, partners, axis=0)
    stacked = with_rotation(partner_blocks, windows, 1)
    flat_table = table.reshape(2 * bin_count, lag_count)
    spectrum = (
        jnp.einsum(
            "nfw,rsdfw->rndsf",
            lax.all_gather(white, "mem", axis=0, tiled=True),
            stacked,
            preferred_element_type=jnp.float32,
        )
        * norm_scale
    )
    spectrum = spectrum.astype(jnp.bfloat16)
    spectrum = spectrum.reshape(
        spectrum.shape[0], spectrum.shape[1], spectrum.shape[2], 2 * bin_count
    )
    correlated = jnp.einsum(
        "rndx,xl->rndl", spectrum, flat_table, preferred_element_type=jnp.float32
    ).astype(jnp.bfloat16)
    return correlated.reshape(
        correlated.shape[0], 1, correlated.shape[1], 1, correlated.shape[2], correlated.shape[3]
    )


def solution(mesh):
    return jax.shard_map(
        shards,
        mesh=mesh,
        in_specs=(P(("grp", "mem"), None, None),),
        out_specs=P(None, "grp", None, "mem", None, None),
        check_vma=False,
    )
```

profile of v0, /device:TPU:1, one launch (start us, length us, event | category | flops | bytes accessed | tf_op | source)
XLA Modules:
  0.0 558.8 jit_solution(15928825194021076410)
XLA Ops:
  6.5 0.0 all-gather.3.cloned.1.call-start
  6.5 1.2 convert_element_type.34
  7.7 0.3 fusion.12
  8.0 0.1 maximum_bitcast_fusion.1
  8.1 2.0 divide_convert_fusion
  10.1 0.0 all-gather.3.cloned.1.call-update
  10.1 0.0 all-gather.5.cloned.1.call-start
  10.2 0.7 all-gather.5.cloned.1.call-update
  10.9 0.1 fusion.27
  11.0 0.1 sine_negate_fusion
  11.2 59.0 %all-gather.3.cloned.1.call-done = bf16[96,64,384]{2,1,0:T(8,128)(2,1)} async-done(((bf16[12,64,384]{2,1,0:T(8,128)(2,1)}), bf16[96,64,384]{2,1,0:T(8,128)(2,1)}) %all-gather.3.cloned.1.call-update) | async-done | bytes 4718608 | tf_op jit(solution)/shard_map/all_gather | solution.py:50
  70.2 5.6 %gather_fusion = bf16[7,12,64,384]{3,2,1,0:T(8,128)(2,1)} fusion(bf16[8,12,64,384]{3,2,1,0:T(8,128)(2,1)} %bitcast.34, s32[1024]{0:T(1024)S(1)} %pad_clamp_fusion), kind=kCustom, calls=%fused_computation | custom fusion | bytes 8257564 | tf_op jit(solution)/shard_map/jit(_take)/gather | solution.py:52
  75.8 2.7 broadcast_select_fusion
  78.5 1.0 slice_negate_fusion
  79.5 0.0 copy-start
  79.5 1.6 maximum_bitcast_fusion
  81.2 0.5 copy-done
  81.7 2.4 bitcast_select_fusion
  84.1 6.4 %pad_maximum_fusion = bf16[7,2,12,64,384]{4,3,2,0,1:T(8,128)(2,1)} fusion(bf16[7,1,12,64,384]{4,3,2,0,1:T(8,128)(2,1)S(1)} %maximum_bitcast_fusion, bf16[7,1,12,64,384]{4,3,2,0,1:T(8,128)(2,1)} %bitcast_select_fusion), kind=kLoop, calls=%fused_computation.10 | loop fusion | flops 4128768 | bytes 16515072 | tf_op jit(solution)/shard_map/stack | solution.py:37
  90.5 389.9 %all-gather.5.cloned.1.call-done = bf16[384,64,384]{2,1,0:T(8,128)(2,1)} async-done(((bf16[12,64,384]{2,1,0:T(8,128)(2,1)}), bf16[384,64,384]{2,1,0:T(8,128)(2,1)}) %all-gather.5.cloned.1.call-update) | async-done | bytes 18874384 | tf_op jit(solution)/shard_map/all_gather | solution.py:58
  480.5 51.0 %fusion = f32[64,7,2,12,384]{4,3,2,1,0:T(8,128)} fusion(bf16[384,64,384,1,1]{2,1,0,3,4:T(8,128)(2,1)} %bitcast.33, bf16[7,2,12,64,384]{4,3,2,0,1:T(8,128)(2,1)} %pad_maximum_fusion), kind=kOutput, calls=%fused_computation.1 | convolution fusion | flops 3170893824 | bytes 43646976 | tf_op jit(solution)/shard_map/nfw,rsdfw->rndsf/dot_general | solution.py:56
  531.5 20.5 %fusion.7 = bf16[7,1,384,1,12,128]{5,2,4,3,1,0:T(8,128)(2,1)} fusion(f32[64,7,2,12,384]{4,3,2,1,0:T(8,128)} %fusion, f32[1,64,128]{2,1,0:T(8,128)S(1)} %get-tuple-element.18, f32[1,64,128]{2,1,0:T(8,128)S(1)} %get-tuple-element.19), kind=kOutput, calls=%fused_computation.9 | convolution fusion | flops 1069400064 | bytes 24838144 | tf_op jit(solution)/shard_map/rndx,xl->rndl/dot_general | solution.py:68
  (6 shorter events, 0.1 us)
Async XLA Ops:
  6.5 63.7 %all-gather.3.cloned.1.call-start = ((), (), s32[]{:S(2)}) async-start(), calls=%async_computation | async-start | bytes 5308416 | tf_op jit(solution)/shard_map/all_gather | solution.py:50
  10.1 470.3 %all-gather.5.cloned.1.call-start = ((), (), s32[]{:S(2)}) async-start(), calls=%async_computation.1 | async-start | bytes 19464192 | tf_op jit(solution)/shard_map/all_gather | solution.py:58
  79.5 2.2 copy-start
Sparse Core Ops, SparseCore 0:
  10.2 59.9 all-gather.2
  72.0 408.4 all-gather.4
where the time goes:
time: 559 us
  waiting for transfers between devices  450 us (81%)
  matrix products  71.5 us (13%)
  other arithmetic  18 us (3%)
  between operations  13.5 us (2%)
  local copies, waits for them, and re-layouts  6.11 us (1%)
    all_gather x1, waiting for transfers between devices, shards(): lax.all_gather(white, 'mem', axis=0, tiled=True)  390 us
    all_gather x1, waiting for transfers between devices, shards(): collected = lax.all_gather(white, 'grp', axis=0, tiled=True)  59 us
    dot_general x1, matrix products, shards(): jnp.einsum('nfw,rsdfw->rndsf', lax.all_gather(white, 'mem', axis=0, tiled...  51 us
    dot_general x1, matrix products, shards(): jnp.einsum('rndx,xl->rndl', spectrum, flat_table, preferred_element_type=...  20.5 us
  transfers between devices with their start and end apart: 2, of which 2 were waited for; matrix products, arithmetic and copies ran while one was open for 4% of the time, Pallas kernels for 0%

commit v1 on v0

--- a/solution.py
+++ b/solution.py
@@ -55,7 +55,9 @@
     spectrum = (
         jnp.einsum(
             "nfw,rsdfw->rndsf",
-            lax.all_gather(white, "mem", axis=0, tiled=True),
+            jnp.concatenate(
+                lax.all_to_all(jnp.stack([white] * lax.axis_size("mem")), "mem", 0, 0), axis=0
+            ),
             stacked,
             preferred_element_type=jnp.float32,
         )

time: 559 us -> 436 us (0.78)
  the two profiles are of different devices: /device:TPU:1 before, /device:TPU:238 now
where the time goes in v1:
time: 436 us; the launch traced here: 435 us
  waiting for transfers between devices  311 us (71%)
  matrix products  71.4 us (16%)
  other arithmetic  17.2 us (4%)
  between operations  13.5 us (3%)
  local copies, waits for them, and re-layouts  13.4 us (3%)
  starting transfers between devices  8.44 us (2%)
    all_to_all x1, waiting for transfers between devices, shards(): lax.all_to_all(jnp.stack([white] * lax.axis_size('mem')), 'mem', 0, 0)  236 us
    all_gather x1, waiting for transfers between devices, shards(): collected = lax.all_gather(white, 'grp', axis=0, tiled=True)  74.7 us
    dot_general x1, matrix products, shards(): jnp.einsum('nfw,rsdfw->rndsf', jnp.concatenate(lax.all_to_all(jnp.stack([...  50.9 us
    dot_general x1, matrix products, shards(): jnp.einsum('rndx,xl->rndl', spectrum, flat_table, preferred_element_type=...  20.5 us
  transfers between devices with their start and end apart: 2, of which 2 were waited for; matrix products, arithmetic and copies ran while one was open for 5% of the time, Pallas kernels for 0%

profile of v1, /device:TPU:238, one launch (start us, length us, event | category | flops | bytes accessed | tf_op | source)
XLA Modules:
  0.0 435.1 jit_solution(5667507665595060588)
XLA Ops:
  6.5 1.2 convert_element_type.34
  7.7 0.3 fusion.12
  8.0 0.1 maximum_bitcast_fusion.1
  8.1 1.2 divide_convert_fusion
  9.3 0.0 copy-start.1
  9.3 7.2 %stack.10 = bf16[32,12,64,384]{3,2,1,0:T(8,128)(2,1)} broadcast(bf16[12,64,384]{2,1,0:T(8,128)(2,1)S(1)} %divide_convert_fusion), dimensions={1,2,3} | broadcast | bytes 19464192 | tf_op jit(solution)/shard_map/stack | solution.py:59
  16.5 0.0 copy-done.1
  16.5 8.4 %all-to-all-start = ((bf16[32,12,64,384]{3,2,1,0:T(8,128)(2,1)}), bf16[32,12,64,384]{3,2,1,0:T(8,128)(2,1)}, u32[]{:S(2)}, u32[]{:S(2)}) async-start(bf16[32,12,64,384]{3,2,1,0:T(8,128)(2,1)} %stack.10), calls=%async_computation | async-start | bytes 37748736 | tf_op jit(solution)/shard_map/all_to_all | solution.py:59
  24.9 0.0 all-gather.2.cloned.1.call-start
  25.0 0.7 all-gather.2.cloned.1.call-update
  25.7 0.1 fusion.27
  25.8 0.1 sine_negate_fusion
  26.0 74.7 %all-gather.2.cloned.1.call-done = bf16[96,64,384]{2,1,0:T(8,128)(2,1)} async-done(((bf16[12,64,384]{2,1,0:T(8,128)(2,1)}), bf16[96,64,384]{2,1,0:T(8,128)(2,1)}) %all-gather.2.cloned.1.call-update) | async-done | bytes 4718608 | tf_op jit(solution)/shard_map/all_gather | solution.py:50
  100.6 5.6 %gather_fusion = bf16[7,12,64,384]{3,2,1,0:T(8,128)(2,1)} fusion(bf16[8,12,64,384]{3,2,1,0:T(8,128)(2,1)} %bitcast.35, s32[1024]{0:T(1024)S(1)} %pad_clamp_fusion), kind=kCustom, calls=%fused_computation | custom fusion | bytes 8257564 | tf_op jit(solution)/shard_map/jit(_take)/gather | solution.py:52
  106.2 2.7 broadcast_select_fusion
  108.9 1.0 slice_negate_fusion
  109.9 0.0 copy-start
  109.9 1.6 maximum_bitcast_fusion
  111.6 0.5 copy-done
  112.1 2.5 bitcast_select_fusion
  114.5 6.4 %pad_maximum_fusion = bf16[7,2,12,64,384]{4,3,2,0,1:T(8,128)(2,1)} fusion(bf16[7,1,12,64,384]{4,3,2,0,1:T(8,128)(2,1)S(1)} %maximum_bitcast_fusion, bf16[7,1,12,64,384]{4,3,2,0,1:T(8,128)(2,1)} %bitcast_select_fusion), kind=kLoop, calls=%fused_computation.10 | loop fusion | flops 4128768 | bytes 16515072 | tf_op jit(solution)/shard_map/stack | solution.py:37
  121.0 235.9 %all-to-all-done = bf16[32,12,64,384]{3,2,1,0:T(8,128)(2,1)} async-done(((bf16[32,12,64,384]{3,2,1,0:T(8,128)(2,1)}), bf16[32,12,64,384]{3,2,1,0:T(8,128)(2,1)}, u32[]{:S(2)}, u32[]{:S(2)}) %all-to-all-start) | async-done | bytes 18874400 | tf_op jit(solution)/shard_map/all_to_all | solution.py:59
  356.9 50.9 %fusion = f32[64,7,2,12,384]{4,3,2,1,0:T(8,128)} fusion(bf16[384,64,384,1,1]{2,1,0,3,4:T(8,128)(2,1)} %bitcast.8, bf16[7,2,12,64,384]{4,3,2,0,1:T(8,128)(2,1)} %pad_maximum_fusion), kind=kOutput, calls=%fused_computation.1 | convolution fusion | flops 3170893824 | bytes 43646976 | tf_op jit(solution)/shard_map/nfw,rsdfw->rndsf/dot_general | solution.py:56
  407.8 20.5 %fusion.7 = bf16[7,1,384,1,12,128]{5,2,4,3,1,0:T(8,128)(2,1)} fusion(f32[64,7,2,12,384]{4,3,2,1,0:T(8,128)} %fusion, f32[1,64,128]{2,1,0:T(8,128)S(1)} %get-tuple-element.18, f32[1,64,128]{2,1,0:T(8,128)S(1)} %get-tuple-element.19), kind=kOutput, calls=%fused_computation.9 | convolution fusion | flops 1069400064 | bytes 24838144 | tf_op jit(solution)/shard_map/rndx,xl->rndl/dot_general | solution.py:70
  (6 shorter events, 0.1 us)
Async XLA Ops:
  9.3 7.2 %copy-start.1 = (bf16[12,64,384]{2,1,0:T(8,128)(2,1)}, bf16[12,64,384]{2,1,0:T(8,128)(2,1)S(1)}, u32[]{:S(2)}) copy-start(bf16[12,64,384]{2,1,0:T(8,128)(2,1)S(1)} %divide_convert_fusion) | copy-start | bytes 1769476
  16.5 340.4 %all-to-all-start = ((bf16[32,12,64,384]{3,2,1,0:T(8,128)(2,1)}), bf16[32,12,64,384]{3,2,1,0:T(8,128)(2,1)}, u32[]{:S(2)}, u32[]{:S(2)}) async-start(bf16[32,12,64,384]{3,2,1,0:T(8,128)(2,1)} %stack.10), calls=%async_computation | async-start | bytes 37748736 | tf_op jit(solution)/shard_map/all_to_all | solution.py:59
  24.9 75.7 %all-gather.2.cloned.1.call-start = ((), (), s32[]{:S(2)}) async-start(), calls=%async_computation.1 | async-start | bytes 5308416 | tf_op jit(solution)/shard_map/all_gather | solution.py:50
  109.9 2.2 copy-start
Sparse Core Ops, SparseCore 0:
  27.6 73.0 all-gather.1
